TPU v7x, 256 devices: a whole 4x4x8 slice. The times are simulated.
256 devices in a mesh: ctx: 8 (over z_lo, core), ep: 32 (over y, x, z_hi).
Axes of the slice: x: 4, y: 4, z: 8 (z_hi: 2, z_lo: 4; z = z_hi * 4 + z_lo), core: 2. Of those that a mesh axis runs over, the one named last changes fastest.
Arguments:
- queries: bfloat16 [32768, 2048], P(('ctx', 'ep')), may hold values from -40 to 40
- keys: bfloat16 [32768, 256], P(('ctx', 'ep')), may hold values from -40 to 40
- values: bfloat16 [32768, 256], P(('ctx', 'ep')), may hold values from -6 to 6
- prior_out: bfloat16 [32768, 2048], P(('ctx', 'ep')), may hold values from -6 to 6
- prior_lse: float32 [32768, 16], P(('ctx', 'ep')), may hold values from 4 to 8
- residual: bfloat16 [32768, 2048], P(('ctx', 'ep')), may hold values from -40 to 40
- out_proj: bfloat16 [2048, 2048], P(('ctx', 'ep')), may hold values from -0.5 to 0.5
- norm_gain: float32 [2048], replicated, may hold values from 0.5 to 1.5
- expert_in: bfloat16 [32, 2048, 1536], P('ep'), may hold values from -0.125 to 0.125
- expert_out: bfloat16 [32, 768, 2048], P('ep'), may hold values from -0.21875 to 0.21875
- expert_ids: int32 [32768, 8], P(('ctx', 'ep')), may hold values from 0 to 31, as said below
- route_weight: float32 [32768, 8], P(('ctx', 'ep')), may hold values from 0.05 to 0.6
Outputs:
- layer_out: bfloat16 [32768, 2048], P(('ctx', 'ep'))
- attended: bfloat16 [32768, 2048], P(('ctx', 'ep'))
Inputs may be any that keep to these rules, and one draw needn't show every extreme that they name: `expert_ids`: each row names 8 different experts. In the rows of one device no expert is named more than 40 times, and one expert is named exactly 40 times in the rows of every device.
All inputs are finite; a program needn't handle non-finite values.
Results may differ from a plain program's by a relative error of at most 0.0061.
Values may be sent and summed in bfloat16 or wider, within the bound.
A program may use at most 128 MiB of HBM per device.

v0:
```python
import math
import jax
import jax.numpy as jnp
from jax import lax
from jax.sharding import PartitionSpec as P

HEADS = 16
KVH = 2
HD = 128
GROUP = 8


def passed_along(shard, axis, by):
    devices = lax.axis_size(axis)
    return lax.ppermute(shard, axis, [(i, (i + by) % devices) for i in range(devices)])


def run_expert(inputs, weight_in, weight_out, hidden_units):
    flat_in = inputs.reshape(-1, inputs.shape[-1])
    gate_up = jnp.dot(flat_in, weight_in, preferred_element_type=jnp.float32)
    activated = (jax.nn.silu(gate_up[:, :hidden_units]) * gate_up[:, hidden_units:]).astype(
        jnp.bfloat16
    )
    replies = jnp.dot(activated, weight_out, preferred_element_type=jnp.float32).astype(
        jnp.bfloat16
    )
    return replies.reshape(inputs.shape[:-1] + (weight_out.shape[-1],))


def shards(
    queries,
    keys,
    values,
    prior_out,
    prior_lse,
    residual,
    out_proj,
    norm_gain,
    expert_in,
    expert_out,
    expert_ids,
    route_weight,
):
    local_rows = queries.shape[0]
    ctx_count = lax.axis_size("ctx")
    ctx_here = lax.axis_index("ctx")
    ep_count = lax.axis_size("ep")
    reach_steps = min(2, ctx_count - 1)
    kv_pair = jnp.stack([keys, values])
    arrived = []
    current = kv_pair
    for stride in range(reach_steps):
        current = passed_along(current, "ctx", 1)
        arrived.append(current)
    window = jnp.concatenate(arrived, axis=1)
    width_kv = window.shape[1]
    key_win = window[0].reshape(width_kv, KVH, HD)
    value_win = window[1].reshape(width_kv, KVH, HD)
    query_blk = queries.reshape(local_rows, KVH, GROUP, HD)
    scores = jnp.einsum(
        "ighd,jgd->ghij", query_blk, key_win, preferred_element_type=jnp.float32
    ) / math.sqrt(HD)
    positions = jnp.arange(width_kv, dtype=jnp.int32)
    key_local = positions % local_rows
    key_ctx = (ctx_here - (positions // local_rows + 1)) % ctx_count
    query_local = jnp.arange(local_rows, dtype=jnp.int32)[:, None]
    visible = (key_local[None, :] < query_local) | (key_local[None, :] == query_local) & (
        key_ctx[None, :] <= ctx_here
    )
    scores = jnp.where(visible, scores, -jnp.inf)
    lse_prior = prior_lse.reshape(local_rows, KVH, GROUP).transpose(1, 2, 0)
    top_score = jnp.maximum(lse_prior, jnp.max(scores, axis=-1))
    weights = jnp.exp(scores - top_score[..., None])
    prior_weight = jnp.exp(lse_prior - top_score)
    totals = prior_weight + jnp.sum(weights, axis=-1)
    gathered = jnp.einsum(
        "ghij,jgd->ighd",
        weights.astype(jnp.bfloat16),
        value_win,
        preferred_element_type=jnp.float32,
    )
    prior_part = (
        prior_out.reshape(local_rows, KVH, GROUP, HD).astype(jnp.float32)
        * prior_weight.transpose(2, 0, 1)[..., None]
    )
    attended = ((prior_part + gathered) / totals.transpose(2, 0, 1)[..., None]).astype(jnp.bfloat16)
    attended = attended.reshape(local_rows, HEADS * HD)
    model_width = out_proj.shape[1]
    column_half = model_width // 2
    core = ctx_here % 2
    column_rows = lax.all_gather(out_proj, "ctx", axis=0, tiled=True)
    own_half = lax.dynamic_slice_in_dim(column_rows, core * column_half, column_half, axis=1)
    own_half = lax.all_gather(own_half, "ep", axis=0, tiled=True)
    other_half = lax.ppermute(own_half, "ctx", [(i, i ^ 1) for i in range(ctx_count)])
    block_rows = out_proj.shape[0]
    attended_perm = (
        attended.reshape(local_rows, ctx_count, ep_count, block_rows)
        .transpose(0, 2, 1, 3)
        .reshape(local_rows, HEADS * HD)
    )
    own_part = jnp.dot(attended_perm, own_half, preferred_element_type=jnp.float32)
    other_part = jnp.dot(attended_perm, other_half, preferred_element_type=jnp.float32)
    projected = jnp.zeros((local_rows, model_width), jnp.float32)
    projected = lax.dynamic_update_slice_in_dim(projected, own_part, core * column_half, axis=1)
    projected = lax.dynamic_update_slice_in_dim(
        projected, other_part, (1 - core) * column_half, axis=1
    )
    mixed_state = (residual.astype(jnp.float32) + projected).astype(jnp.bfloat16)
    state_f = lax.optimization_barrier(mixed_state).astype(jnp.float32)
    normed = (
        state_f * lax.rsqrt(jnp.mean(state_f * state_f, axis=-1, keepdims=True) + 1e-06) * norm_gain
    ).astype(jnp.bfloat16)
    experts_all = ep_count * expert_in.shape[0]
    top_count = expert_ids.shape[1]
    capacity = max(
        local_rows // 4, top_count * ((local_rows + experts_all - 2) // (experts_all - 1))
    )
    flat_ids = expert_ids.reshape(-1)
    one_hot = (flat_ids[:, None] == jnp.arange(experts_all, dtype=jnp.int32)[None, :]).astype(
        jnp.int32
    )
    earlier = jnp.cumsum(one_hot, axis=0) - one_hot
    slot_ids = flat_ids * capacity + jnp.sum(earlier * one_hot, axis=1)
    outgoing = jnp.zeros((experts_all * capacity, model_width), jnp.bfloat16)
    outgoing = (
        outgoing.at[slot_ids]
        .set(jnp.repeat(normed, top_count, axis=0))
        .reshape(experts_all, capacity, model_width)
    )
    weight_in = expert_in[0]
    weight_out = expert_out[0]
    hidden_units = weight_out.shape[0]
    replies = run_expert(
        lax.all_to_all(outgoing, "ep", split_axis=0, concat_axis=0, tiled=True),
        weight_in,
        weight_out,
        hidden_units,
    )
    returned = lax.all_to_all(replies, "ep", split_axis=0, concat_axis=0, tiled=True)
    picked = returned.reshape(experts_all * capacity, model_width)[slot_ids].reshape(
        local_rows, top_count, model_width
    )
    combined = jnp.sum(route_weight[:, :, None] * picked.astype(jnp.float32), axis=1)
    layer_out = (state_f + combined).astype(jnp.bfloat16)
    return (layer_out, attended)


def solution(mesh):
    return jax.shard_map(
        shards,
        mesh=mesh,
        in_specs=(
            P(("ctx", "ep"), None),
            P(("ctx", "ep"), None),
            P(("ctx", "ep"), None),
            P(("ctx", "ep"), None),
            P(("ctx", "ep"), None),
            P(("ctx", "ep"), None),
            P(("ctx", "ep"), None),
            P(),
            P("ep", None, None),
            P("ep", None, None),
            P(("ctx", "ep"), None),
            P(("ctx", "ep"), None),
        ),
        out_specs=(P(("ctx", "ep"), None), P(("ctx", "ep"), None)),
        check_vma=False,
    )
```

profile of v0, /device:TPU:94, one launch (start us, length us, event | category | flops | bytes accessed | tf_op | source)
XLA Modules:
  0.0 471.1 jit_solution(506274494953376835)
XLA Ops:
  7.2 12.8 %all_gather.6 = bf16[64,2048]{1,0:T(8,128)(2,1)S(1)} all-gather(bf16[8,2048]{1,0:T(8,128)(2,1)} %param.18), channel_id=1, replica_groups=mesh['ctx'=8,'ep'=32] {'ctx'}, dimensions={0}, use_global_device_ids=true | all-gather | bytes 294912 | tf_op jit(solution)/shard_map/all_gather | solution.py:91
  20.1 0.7 constant_dynamic-slice_fusion
  20.8 111.6 %all-gather.2.cloned.1.call-done = bf16[2048,1024]{1,0:T(8,128)(2,1)} async-done(((bf16[64,1024]{1,0:T(8,128)(2,1)}), bf16[2048,1024]{1,0:T(8,128)(2,1)}) %all-gather.2.cloned.1.call-update) | async-done | bytes 4194320 | tf_op jit(solution)/shard_map/all_gather | solution.py:93
  132.4 0.9 copy.21
  133.3 1.0 copy.22
  134.3 0.7 pad_maximum_fusion
  135.0 0.5 collective-permute-start
  135.5 0.8 copy.29
  136.4 9.0 %reduce-window.6 = s32[32,8,128]{2,1,0:T(8,128)S(1)} reduce-window(s32[32,8,128]{2,1,0:T(8,128)S(1)} %fusion.28, s32[]{:T(128)} %constant.73.clone.1), window={size=1x1x128 pad=0_0x0_0x127_0}, to_apply=%region_2.3 | reduce-window | flops 4161536 | bytes 262148 | tf_op jit(solution)/shard_map/reduce-window
  146.0 0.7 broadcast_multiply_fusion
  147.2 2.0 copy.39
  149.1 2.3 copy.20
  151.5 1.0 constant_dynamic-update-slice_fusion.1
  152.5 1.6 fusion.38
  154.1 0.3 fusion.11
  154.5 0.5 fusion.15
  155.2 0.7 copy-done.4
  156.0 0.9 copy-done.3
  156.8 0.7 convolution_dynamic-update-slice_fusion.1
  157.6 3.0 convolution_dynamic-update-slice_fusion
  160.9 0.6 copy-done.1
  161.5 1.0 fusion.18
  162.5 10.1 %scatter_custom_fusion = bf16[1280,2048]{1,0:T(8,128)(2,1)} fusion(s32[1024]{0:T(1024)S(1)} %bitcast.102, bf16[]{:T(256)} %constant.86.clone.1, bf16[128,2048]{1,0:T(8,128)(2,1)} %fusion.18), kind=kCustom, calls=%fused_computation.7 | custom fusion | bytes 5767170 | tf_op jit(solution)/shard_map/scatter | solution.py:127
  172.5 127.9 %all_to_all.10 = bf16[32,40,2048]{2,1,0:T(8,128)(2,1)S(1)} all-to-all(bf16[32,40,2048]{2,1,0:T(8,128)(2,1)} %bitcast.85), channel_id=1, replica_groups=mesh['ctx'=8,'ep'=32] {'ep'}, dimensions={0} | all-to-all | bytes 10485760 | tf_op jit(solution)/shard_map/all_to_all | solution.py:134
  300.4 10.5 %fusion.1 = f32[1280,1536]{1,0:T(8,128)S(1)} fusion(bf16[1280,2048]{1,0:T(8,128)(2,1)S(1)} %bitcast.87, bf16[1,2048,1536]{2,1,0:T(8,128)(2,1)} %param.20), kind=kOutput, calls=%fused_computation.5 | convolution fusion | flops 8053063680 | bytes 19398656 | tf_op jit(solution)/shard_map/dot_general | solution.py:20
  311.0 6.1 %convolution_convert_fusion = bf16[1280,2048]{1,0:T(8,128)(2,1)} fusion(bf16[1,768,2048]{2,1,0:T(8,128)(2,1)S(1)} %copy-done, f32[1280,1536]{1,0:T(8,128)S(1)} %fusion.1), kind=kOutput, calls=%fused_computation.4 | convolution fusion | flops 4035051520 | bytes 16252928 | tf_op jit(solution)/shard_map/dot_general | solution.py:24
  317.1 8.9 %all-to-all-start.1 = ((bf16[32,40,2048]{2,1,0:T(8,128)(2,1)}), bf16[32,40,2048]{2,1,0:T(8,128)(2,1)}, u32[]{:S(2)}, u32[]{:S(2)}) async-start(bf16[32,40,2048]{2,1,0:T(8,128)(2,1)} %bitcast.86), calls=%async_computation.1 | async-start | bytes 10485760 | tf_op jit(solution)/shard_map/all_to_all | solution.py:139
  326.0 2.0 copy.33
  328.1 116.6 %all-to-all-done.1 = bf16[32,40,2048]{2,1,0:T(8,128)(2,1)} async-done(((bf16[32,40,2048]{2,1,0:T(8,128)(2,1)}), bf16[32,40,2048]{2,1,0:T(8,128)(2,1)}, u32[]{:S(2)}, u32[]{:S(2)}) %all-to-all-start.1) | async-done | bytes 5242912 | tf_op jit(solution)/shard_map/all_to_all | solution.py:139
  444.7 12.0 %gather_fusion = bf16[1024,2048]{1,0:T(8,128)(2,1)} fusion(bf16[1280,2048]{1,0:T(8,128)(2,1)} %bitcast.28, s32[1024]{0:T(1024)S(1)} %broadcast_clamp_fusion), kind=kCustom, calls=%fused_computation | custom fusion | bytes 8392704 | tf_op jit(solution)/shard_map/gather | solution.py:140
  456.7 6.6 %fusion = f32[128,2048]{1,0:T(8,128)S(1)} fusion(bf16[1024,2048]{1,0:T(8,128)(2,1)} %gather_fusion, f32[128,8]{1,0:T(8,128)S(1)} %copy.27), kind=kLoop, calls=%fused_computation.3 | loop fusion | flops 6029312 | bytes 5246976 | tf_op jit(solution)/shard_map/reduce_sum | solution.py:143
  463.3 0.9 fusion.19
  (51 shorter events, 1.9 us)
Async XLA Ops:
  7.2 303.8 %copy-start = (bf16[1,768,2048]{2,1,0:T(8,128)(2,1)S(1)}, bf16[1,768,2048]{2,1,0:T(8,128)(2,1)}, u32[]{:S(2)}) copy-start(bf16[1,768,2048]{2,1,0:T(8,128)(2,1)} %param.21) | copy-start | bytes 9437188
  7.2 125.2 %all-gather.2.cloned.1.call-start = ((), (), s32[]{:S(2)}) async-start(), calls=%async_computation.2 | async-start | bytes 4325376 | tf_op jit(solution)/shard_map/all_gather | solution.py:93
  132.4 25.2 %collective-permute-start.2 = (bf16[2048,1024]{1,0:T(8,128)(2,1)}, bf16[2048,1024]{1,0:T(8,128)(2,1)}, u32[]{:S(2)}, u32[]{:S(2)}) collective-permute-start(bf16[2048,1024]{1,0:T(8,128)(2,1)} %all-gather.2.cloned.1.call-done), channel_id=1, source_target_pairs={{0,32},{32,0},{64,96},{96,64},{128,160},{160,128},{192,224},{224,1... | collective-permute-start | bytes 12582920 | tf_op jit(solution)/shard_map/ppermute | solution.py:94
  134.3 19.8 %copy-start.7 = (f32[128,16]{0,1:T(8,128)S(1)}, f32[128,16]{0,1:T(8,128)}, u32[]{:S(2)}) copy-start(f32[128,16]{0,1:T(8,128)} %param.16) | copy-start | bytes 24580
  135.0 12.1 %collective-permute-start = (bf16[2,128,256]{1,2,0:T(8,128)(2,1)}, bf16[2,128,256]{1,2,0:T(8,128)(2,1)}, u32[]{:S(2)}, u32[]{:S(2)}) collective-permute-start(bf16[2,128,256]{1,2,0:T(8,128)(2,1)} %pad_maximum_fusion), channel_id=1, source_target_pairs={{0,32},{32,64},{64,96},{96,128},{128,160},{160,192},{192,224},{224... | collective-permute-start | bytes 393224 | tf_op jit(solution)/shard_map/ppermute | solution.py:15
  147.1 5.4 %collective-permute-start.1 = (bf16[2,128,256]{1,2,0:T(8,128)(2,1)}, bf16[2,128,256]{1,2,0:T(8,128)(2,1)S(1)}, u32[]{:S(2)}, u32[]{:S(2)}) collective-permute-start(bf16[2,128,256]{1,2,0:T(8,128)(2,1)} %collective-permute-done), channel_id=1, source_target_pairs={{0,32},{32,64},{64,96},{96,128},{128,160},{160,192},{192,224},{224... | collective-permute-start | bytes 393224 | tf_op jit(solution)/shard_map/ppermute | solution.py:15
  151.4 3.0 copy-start.5
  154.5 2.4 copy-start.3
  155.0 0.8 copy-start.4
  156.8 3.7 copy-start.6
  157.6 3.9 copy-start.8
  160.7 0.8 copy-start.1
  317.1 8.9 %copy-start.9 = (f32[128,8]{0,1:T(8,128)S(1)}, f32[128,8]{0,1:T(8,128)}, u32[]{:S(2)}) copy-start(f32[128,8]{0,1:T(8,128)} %param.23) | copy-start | bytes 12292
  317.1 127.6 %all-to-all-start.1 = ((bf16[32,40,2048]{2,1,0:T(8,128)(2,1)}), bf16[32,40,2048]{2,1,0:T(8,128)(2,1)}, u32[]{:S(2)}, u32[]{:S(2)}) async-start(bf16[32,40,2048]{2,1,0:T(8,128)(2,1)} %bitcast.86), calls=%async_computation.1 | async-start | bytes 10485760 | tf_op jit(solution)/shard_map/all_to_all | solution.py:139
  456.7 6.6 %copy-start.2 = (bf16[128,2048]{1,0:T(8,128)(2,1)S(1)}, bf16[128,2048]{1,0:T(8,128)(2,1)}, u32[]{:S(2)}) copy-start(bf16[128,2048]{1,0:T(8,128)(2,1)} %copy-done.1) | copy-start | bytes 1572868
Sparse Core Ops, SparseCore 0:
  20.9 111.4 all-gather.1
where the time goes:
time: 472 us; the launch traced here: 471 us
  waiting for transfers between devices  228 us (48%)
  blocking collectives  141 us (30%)
  local copies, waits for them, and re-layouts  36 us (8%)
  matrix products  22.4 us (5%)
  other arithmetic  19.8 us (4%)
  between operations  14.4 us (3%)
  starting transfers between devices  9.49 us (2%)
    all_to_all x1, blocking collectives, shards(): lax.all_to_all(outgoing, 'ep', split_axis=0, concat_axis=0, tiled=True)  128 us
    all_to_all x1, waiting for transfers between devices, shards(): lax.all_to_all(replies, 'ep', split_axis=0, concat_axis=0, tiled=True)  117 us
    all_gather x1, waiting for transfers between devices, shards(): own_half = lax.all_gather(own_half, 'ep', axis=0, tiled=True)  112 us
    all_gather x1, blocking collectives, shards(): column_rows = lax.all_gather(out_proj, 'ctx', axis=0, tiled=True)  12.8 us
    gather x1, local copies, waits for them, and re-layouts, shards(): returned.reshape(experts_all * capacity, model_width)[slot_ids]  12 us
    dot_general x1, matrix products, run_expert(): gate_up = jnp.dot(flat_in, weight_in, preferred_element_type=jnp.float32)  10.5 us
    scatter x1, local copies, waits for them, and re-layouts, shards(): outgoing = outgoing.at[slot_ids].set(jnp.repeat(normed, top_count, axis=0...  10.1 us
    unnamed x27, local copies, waits for them, and re-layouts  9.98 us
  transfers between devices with their start and end apart: 5, of which 2 were waited for; matrix products, arithmetic and copies ran while one was open for 5% of the time, Pallas kernels for 0%

commit v1 on v0

--- a/solution.py
+++ b/solution.py
@@ -41,6 +41,14 @@
     expert_ids,
     route_weight,
 ):
+
+    def sources_all_view(group_axis, x_part):
+        val2 = lax.axis_size(group_axis)
+        before = jnp.stack([x_part] * val2)
+        arr_now = lax.all_to_all(before, group_axis, 0, 0)
+        w_next = jnp.concatenate(arr_now, axis=0)
+        return w_next
+
     local_rows = queries.shape[0]
     ctx_count = lax.axis_size("ctx")
     ctx_here = lax.axis_index("ctx")
@@ -90,7 +98,7 @@
     core = ctx_here % 2
     column_rows = lax.all_gather(out_proj, "ctx", axis=0, tiled=True)
     own_half = lax.dynamic_slice_in_dim(column_rows, core * column_half, column_half, axis=1)
-    own_half = lax.all_gather(own_half, "ep", axis=0, tiled=True)
+    own_half = sources_all_view("ep", own_half)
     other_half = lax.ppermute(own_half, "ctx", [(i, i ^ 1) for i in range(ctx_count)])
     block_rows = out_proj.shape[0]
     attended_perm = (

time: 472 us -> 458 us (0.970)
  the two profiles are of different devices: /device:TPU:94 before, /device:TPU:96 now
where the time goes in v1:
time: 458 us; the launch traced here: 457 us
  blocking collectives  253 us (55%)
  waiting for transfers between devices  120 us (26%)
  local copies, waits for them, and re-layouts  31.8 us (7%)
  matrix products  24.7 us (5%)
  other arithmetic  19.1 us (4%)
  starting transfers between devices  7.22 us (2%)
    all_to_all x1, blocking collectives, shards(): lax.all_to_all(outgoing, 'ep', split_axis=0, concat_axis=0, tiled=True)  127 us
    all_to_all x1, waiting for transfers between devices, shards(): lax.all_to_all(replies, 'ep', split_axis=0, concat_axis=0, tiled=True)  120 us
    all_to_all x1, blocking collectives, sources_all_view(): arr_now = lax.all_to_all(before, group_axis, 0, 0)  111 us
    all_gather x1, blocking collectives, shards(): column_rows = lax.all_gather(out_proj, 'ctx', axis=0, tiled=True)  14.6 us
    gather x1, local copies, waits for them, and re-layouts, shards(): returned.reshape(experts_all * capacity, model_width)[slot_ids]  12.2 us
    dot_general x1, matrix products, run_expert(): gate_up = jnp.dot(flat_in, weight_in, preferred_element_type=jnp.float32)  10.5 us
    scatter x1, local copies, waits for them, and re-layouts, shards(): outgoing = outgoing.at[slot_ids].set(jnp.repeat(normed, top_count, axis=0...  10.1 us
  transfers between devices with their start and end apart: 4, of which 1 were waited for; matrix products, arithmetic and copies ran while one was open for 5% of the time, Pallas kernels for 0%

profile of v1, /device:TPU:96, one launch (start us, length us, event | category | flops | bytes accessed | tf_op | source)
XLA Modules:
  0.0 457.3 jit_solution(1143000788525104983)
XLA Ops:
  0.7 14.6 %all_gather.3 = bf16[64,2048]{1,0:T(8,128)(2,1)S(1)} all-gather(bf16[8,2048]{1,0:T(8,128)(2,1)} %param.18), channel_id=1, replica_groups=mesh['ctx'=8,'ep'=32] {'ctx'}, dimensions={0}, use_global_device_ids=true | all-gather | bytes 294912 | tf_op jit(solution)/shard_map/all_gather | solution.py:99
  15.2 0.5 stack.11
  15.8 111.4 %all_to_all.15 = bf16[32,64,1024]{2,1,0:T(8,128)(2,1)} all-to-all(bf16[32,64,1024]{2,1,0:T(8,128)(2,1)S(1)} %stack.11), channel_id=1, replica_groups=mesh['ctx'=8,'ep'=32] {'ep'}, dimensions={0} | all-to-all | bytes 8388608 | tf_op jit(solution)/shard_map/all_to_all | solution.py:48
  127.5 0.7 pad_maximum_fusion
  128.2 0.5 collective-permute-start
  128.9 9.0 %reduce-window.6 = s32[32,8,128]{2,1,0:T(8,128)S(1)} reduce-window(s32[32,8,128]{2,1,0:T(8,128)S(1)} %fusion.28, s32[]{:T(128)} %constant.73.clone.1), window={size=1x1x128 pad=0_0x0_0x127_0}, to_apply=%region_2.3 | reduce-window | flops 4161536 | bytes 262148 | tf_op jit(solution)/shard_map/reduce-window
  138.0 0.1 copy.31
  138.3 0.1 fusion.26
  138.9 1.7 collective-permute-start.1
  140.6 2.0 copy.39
  142.6 2.3 copy.20
  144.9 1.0 constant_dynamic-update-slice_fusion.1
  146.0 1.6 fusion.38
  147.6 0.3 fusion.11
  147.9 0.5 fusion.15
  148.5 0.1 copy.26
  148.6 0.7 copy-done.4
  149.4 3.0 convolution_dynamic-update-slice_fusion.1
  152.4 2.9 convolution_dynamic-update-slice_fusion
  155.5 0.2 fusion.16
  155.7 0.6 copy-done.2
  156.3 1.0 fusion.18
  157.3 10.1 %scatter_custom_fusion = bf16[1280,2048]{1,0:T(8,128)(2,1)} fusion(s32[1024]{0:T(1024)S(1)} %bitcast.103, bf16[]{:T(256)} %constant.86.clone.1, bf16[128,2048]{1,0:T(8,128)(2,1)} %fusion.18), kind=kCustom, calls=%fused_computation.7 | custom fusion | bytes 5767170 | tf_op jit(solution)/shard_map/scatter | solution.py:135
  167.3 127.4 %all_to_all.16 = bf16[32,40,2048]{2,1,0:T(8,128)(2,1)S(1)} all-to-all(bf16[32,40,2048]{2,1,0:T(8,128)(2,1)} %bitcast.86), channel_id=1, replica_groups=mesh['ctx'=8,'ep'=32] {'ep'}, dimensions={0} | all-to-all | bytes 10485760 | tf_op jit(solution)/shard_map/all_to_all | solution.py:142
  294.8 10.5 %fusion.1 = f32[1280,1536]{1,0:T(8,128)S(1)} fusion(bf16[1280,2048]{1,0:T(8,128)(2,1)S(1)} %bitcast.88, bf16[1,2048,1536]{2,1,0:T(8,128)(2,1)} %param.20), kind=kOutput, calls=%fused_computation.5 | convolution fusion | flops 8053063680 | bytes 19398656 | tf_op jit(solution)/shard_map/dot_general | solution.py:20
  305.3 6.1 %convolution_convert_fusion = bf16[1280,2048]{1,0:T(8,128)(2,1)} fusion(bf16[1,768,2048]{2,1,0:T(8,128)(2,1)S(1)} %copy-done, f32[1280,1536]{1,0:T(8,128)S(1)} %fusion.1), kind=kOutput, calls=%fused_computation.4 | convolution fusion | flops 4035051520 | bytes 16252928 | tf_op jit(solution)/shard_map/dot_general | solution.py:24
  311.4 5.0 %all-to-all-start.2 = ((bf16[32,40,2048]{2,1,0:T(8,128)(2,1)}), bf16[32,40,2048]{2,1,0:T(8,128)(2,1)}, u32[]{:S(2)}, u32[]{:S(2)}) async-start(bf16[32,40,2048]{2,1,0:T(8,128)(2,1)} %bitcast.87), calls=%async_computation.2 | async-start | bytes 10485760 | tf_op jit(solution)/shard_map/all_to_all | solution.py:147
  316.5 1.0 copy.33
  317.6 120.1 %all-to-all-done.2 = bf16[32,40,2048]{2,1,0:T(8,128)(2,1)} async-done(((bf16[32,40,2048]{2,1,0:T(8,128)(2,1)}), bf16[32,40,2048]{2,1,0:T(8,128)(2,1)}, u32[]{:S(2)}, u32[]{:S(2)}) %all-to-all-start.2) | async-done | bytes 5242912 | tf_op jit(solution)/shard_map/all_to_all | solution.py:147
  437.6 12.2 %gather_fusion = bf16[1024,2048]{1,0:T(8,128)(2,1)} fusion(bf16[1280,2048]{1,0:T(8,128)(2,1)} %bitcast.29, s32[1024]{0:T(1024)S(1)} %broadcast_clamp_fusion), kind=kCustom, calls=%fused_computation | custom fusion | bytes 8392704 | tf_op jit(solution)/shard_map/gather | solution.py:148
  449.8 6.6 %fusion = f32[128,2048]{1,0:T(8,128)S(1)} fusion(bf16[1024,2048]{1,0:T(8,128)(2,1)} %gather_fusion, f32[128,8]{1,0:T(8,128)S(1)} %copy.27), kind=kLoop, calls=%fused_computation.3 | loop fusion | flops 6029312 | bytes 5246976 | tf_op jit(solution)/shard_map/reduce_sum | solution.py:151
  456.4 0.9 fusion.19
  (58 shorter events, 1.6 us)
Async XLA Ops:
  0.6 304.7 %copy-start = (bf16[1,768,2048]{2,1,0:T(8,128)(2,1)S(1)}, bf16[1,768,2048]{2,1,0:T(8,128)(2,1)}, u32[]{:S(2)}) copy-start(bf16[1,768,2048]{2,1,0:T(8,128)(2,1)} %param.21) | copy-start | bytes 9437188
  15.8 111.4 %copy-start.8 = (bf16[128,256]{1,0:T(8,128)(2,1)S(1)}, bf16[128,256]{1,0:T(8,128)(2,1)}, u32[]{:S(2)}) copy-start(bf16[128,256]{1,0:T(8,128)(2,1)} %param.13) | copy-start | bytes 196612
  15.8 111.6 %copy-start.9 = (bf16[128,256]{1,0:T(8,128)(2,1)S(1)}, bf16[128,256]{1,0:T(8,128)(2,1)}, u32[]{:S(2)}) copy-start(bf16[128,256]{1,0:T(8,128)(2,1)} %param.14) | copy-start | bytes 196612
  15.8 112.9 %copy-start.11 = (s32[128,8]{0,1:T(8,128)S(1)}, s32[128,8]{0,1:T(8,128)}, u32[]{:S(2)}) copy-start(s32[128,8]{0,1:T(8,128)} %param.22) | copy-start | bytes 12292
  127.2 25.2 %collective-permute-start.2 = (bf16[2048,1024]{1,0:T(8,128)(2,1)}, bf16[2048,1024]{1,0:T(8,128)(2,1)}, u32[]{:S(2)}, u32[]{:S(2)}) collective-permute-start(bf16[2048,1024]{1,0:T(8,128)(2,1)} %bitcast.17), channel_id=1, source_target_pairs={{0,32},{32,0},{64,96},{96,64},{128,160},{160,128},{192,224},{224,1... | collective-permute-start | bytes 12582920 | tf_op jit(solution)/shard_map/ppermute | solution.py:102
  127.5 20.1 %copy-start.10 = (f32[128,16]{0,1:T(8,128)S(1)}, f32[128,16]{0,1:T(8,128)}, u32[]{:S(2)}) copy-start(f32[128,16]{0,1:T(8,128)} %param.16) | copy-start | bytes 24580
  128.2 10.7 %collective-permute-start = (bf16[2,128,256]{1,2,0:T(8,128)(2,1)}, bf16[2,128,256]{1,2,0:T(8,128)(2,1)}, u32[]{:S(2)}, u32[]{:S(2)}) collective-permute-start(bf16[2,128,256]{1,2,0:T(8,128)(2,1)} %pad_maximum_fusion), channel_id=1, source_target_pairs={{0,32},{32,64},{64,96},{96,128},{128,160},{160,192},{192,224},{224... | collective-permute-start | bytes 393224 | tf_op jit(solution)/shard_map/ppermute | solution.py:15
  138.9 7.0 %collective-permute-start.1 = (bf16[2,128,256]{1,2,0:T(8,128)(2,1)}, bf16[2,128,256]{1,2,0:T(8,128)(2,1)S(1)}, u32[]{:S(2)}, u32[]{:S(2)}) collective-permute-start(bf16[2,128,256]{1,2,0:T(8,128)(2,1)} %collective-permute-done), channel_id=1, source_target_pairs={{0,32},{32,64},{64,96},{96,128},{128,160},{160,192},{192,224},{224... | collective-permute-start | bytes 393224 | tf_op jit(solution)/shard_map/ppermute | solution.py:15
  144.9 3.0 copy-start.6
  148.5 0.8 copy-start.4
  149.4 6.0 %copy-start.7 = (bf16[128,2048]{1,0:T(8,128)(2,1)S(1)}, bf16[128,2048]{1,0:T(8,128)(2,1)}, u32[]{:S(2)}) copy-start(bf16[128,2048]{1,0:T(8,128)(2,1)} %param.17) | copy-start | bytes 1572868
  152.4 3.9 copy-start.12
  155.5 0.8 copy-start.2
  311.4 5.0 %copy-start.13 = (f32[128,8]{0,1:T(8,128)S(1)}, f32[128,8]{0,1:T(8,128)}, u32[]{:S(2)}) copy-start(f32[128,8]{0,1:T(8,128)} %param.23) | copy-start | bytes 12292
  311.4 5.1 %copy-start.5 = (bf16[128,2,8,128]{0,3,2,1:T(8,128)(2,1)S(1)}, bf16[128,2,8,128]{0,3,2,1:T(8,128)(2,1)}, u32[]{:S(2)}) copy-start(bf16[128,2,8,128]{0,3,2,1:T(8,128)(2,1)} %copy-done.4) | copy-start | bytes 1572868
  311.4 126.2 %all-to-all-start.2 = ((bf16[32,40,2048]{2,1,0:T(8,128)(2,1)}), bf16[32,40,2048]{2,1,0:T(8,128)(2,1)}, u32[]{:S(2)}, u32[]{:S(2)}) async-start(bf16[32,40,2048]{2,1,0:T(8,128)(2,1)} %bitcast.87), calls=%async_computation.2 | async-start | bytes 10485760 | tf_op jit(solution)/shard_map/all_to_all | solution.py:147
  437.6 19.7 %copy-start.1 = (bf16[1,768,2048]{2,1,0:T(8,128)(2,1)S(1)}, bf16[1,768,2048]{2,1,0:T(8,128)(2,1)}, u32[]{:S(2)}) copy-start(bf16[1,768,2048]{2,1,0:T(8,128)(2,1)} %param.21) | copy-start | bytes 9437188
  449.8 6.6 %copy-start.3 = (bf16[128,2048]{1,0:T(8,128)(2,1)S(1)}, bf16[128,2048]{1,0:T(8,128)(2,1)}, u32[]{:S(2)}) copy-start(bf16[128,2048]{1,0:T(8,128)(2,1)} %copy-done.2) | copy-start | bytes 1572868
